TPU v7x, 512 devices: a whole 4x8x8 slice. The times are simulated.
512 devices in a mesh: rep: 64 (over x, y, core), tp: 8 (over z).
Axes of the slice: x: 4, y: 8, z: 8, core: 2. Of those that a mesh axis runs over, the one named last changes fastest.
Arguments:
- queries: bfloat16 [4096, 2, 8192], P('rep', None, 'tp'), may hold values from -170 to 170
- step_keys: bfloat16 [4096, 2, 1024], P('rep', None, 'tp'), may hold values from -9 to 9
- step_values: bfloat16 [4096, 2, 1024], P('rep', None, 'tp'), may hold values from -6 to 6
- suffix_keys: bfloat16 [4096, 64, 1024], P('rep', None, 'tp'), may hold values from -6 to 6
- suffix_values: bfloat16 [4096, 64, 1024], P('rep', None, 'tp'), may hold values from -6 to 6
- suffix_len: int32 [4096], P('rep'), may hold values from 1 to 64, as said below
- row_schema: int32 [4096], P('rep'), may hold values from 0 to 63, as said below
- held: int32 [64, 2], P('rep'), may hold values from 0 to 63, as said below
- dest_replica: int32 [4096], P('rep'), may hold values from 0 to 63, as said below
- dest_slot: int32 [4096], P('rep'), may hold values from 0 to 63, as said below
- prefix_keys: bfloat16 [64, 2, 2048, 1024], P('rep', None, 'tp'), may hold values from -6 to 6, as said below
- prefix_values: bfloat16 [64, 2, 2048, 1024], P('rep', None, 'tp'), may hold values from -6 to 6, as said below
Outputs:
- attended: bfloat16 [4096, 2, 8192], P('rep', None, 'tp')
Inputs may be any that keep to these rules, and one draw needn't show every extreme that they name: Each schema stands in exactly 2 rows of held, never twice in one row. row_schema[r] is one of the schemas in held[dest_replica[r]]. `dest_replica`: every replica receives exactly 64 rows; of the rows of one replica at most 2 go to one replica, and every replica sends exactly 2 to some replica. The pairs (dest_replica, dest_slot) are all different. `suffix_len`: on every replica some row has exactly 64. `prefix_keys`: copies of one schema on different replicas are equal. `prefix_values`: copies of one schema on different replicas are equal.
All inputs are finite; a program needn't handle non-finite values.
Results may differ from a plain program's by a relative error of at most 0.0035.
Values may be sent and summed in bfloat16 or wider, within the bound.
A program may use at most 128 MiB of HBM per device.

v0:
```python
import jax
import jax.numpy as jnp
from jax import lax
from jax.sharding import PartitionSpec as P

HD = 128


def local_scores(query_rows, key_rows, lengths, suffix_count):
    row_count, step_count, width = query_rows.shape
    kv_count = key_rows.shape[2] // HD
    group_size = width // HD // kv_count
    query_heads = query_rows.reshape(row_count, step_count, kv_count, group_size, HD)
    key_heads = key_rows.reshape(row_count, key_rows.shape[1], kv_count, HD)
    scores = jnp.einsum(
        "rtkgd,rjkd->rtkgj", query_heads, key_heads, preferred_element_type=jnp.float32
    ) * HD ** (-0.5)
    position = jnp.arange(key_rows.shape[1])[None, None, :]
    step_index = jnp.arange(step_count)[None, :, None]
    allowed = (position < suffix_count) & (position < lengths[:, None, None]) | (
        position >= suffix_count
    ) & (position - suffix_count <= step_index)
    return jnp.where(allowed[:, :, None, None, :], scores, -jnp.inf)


def local_sums(scores, row_peak, value_rows):
    kv_count = scores.shape[2]
    weights = jnp.exp(scores - row_peak[..., None]).astype(jnp.bfloat16)
    value_heads = value_rows.reshape(value_rows.shape[0], value_rows.shape[1], kv_count, HD)
    weighted = jnp.einsum(
        "rtkgj,rjkd->rtkgd", weights, value_heads, preferred_element_type=jnp.float32
    )
    totals = jnp.sum(weights.astype(jnp.float32), axis=-1)
    return (weighted, totals)


def prefix_scores(query_rows, prefix_block, chosen):
    row_count, step_count, width = query_rows.shape
    kv_count = prefix_block.shape[2] // HD
    group_size = width // HD // kv_count
    query_heads = query_rows.reshape(row_count, step_count, kv_count, group_size, HD)
    combined = None
    for slot_index in range(prefix_block.shape[0]):
        key_heads = prefix_block[slot_index].reshape(prefix_block.shape[1], kv_count, HD)
        scores = jnp.einsum(
            "rtkgd,pkd->rtkgp", query_heads, key_heads, preferred_element_type=jnp.float32
        ) * HD ** (-0.5)
        if combined is None:
            combined = scores
        else:
            combined = jnp.where(chosen[:, slot_index][:, None, None, None, None], scores, combined)
    return combined


def prefix_sums(scores, row_peak, value_block, chosen):
    kv_count = value_block.shape[2] // HD
    weights = jnp.exp(scores - row_peak[..., None]).astype(jnp.bfloat16)
    totals = jnp.sum(weights.astype(jnp.float32), axis=-1)
    weighted = None
    for slot_index in range(value_block.shape[0]):
        value_heads = value_block[slot_index].reshape(value_block.shape[1], kv_count, HD)
        masked = jnp.where(
            chosen[:, slot_index][:, None, None, None, None], weights, jnp.zeros_like(weights)
        )
        term = jnp.einsum(
            "rtkgp,pkd->rtkgd", masked, value_heads, preferred_element_type=jnp.float32
        )
        weighted = term if weighted is None else weighted + term
    return (weighted, totals)


def shards(
    queries,
    step_keys,
    step_values,
    suffix_keys,
    suffix_values,
    suffix_len,
    row_schema,
    held,
    dest_replica,
    dest_slot,
    prefix_keys,
    prefix_values,
):
    row_count = queries.shape[0]
    replicas = lax.axis_size("rep")
    capacity = 2 * row_count // replicas
    buffer_rows = replicas * capacity
    suffix_count = suffix_keys.shape[1]
    kv_local = step_keys.shape[2] // HD
    tp_index = lax.axis_index("tp")
    row_order = jnp.arange(row_count)
    earlier = (dest_replica[None, :] == dest_replica[:, None]) & (
        row_order[None, :] < row_order[:, None]
    )
    placed = dest_replica * capacity + jnp.sum(earlier.astype(jnp.int32), axis=1)

    def packed(values):
        return jnp.zeros((buffer_rows,) + values.shape[1:], values.dtype).at[placed].set(values)

    prefix_key_rows, prefix_value_rows = (prefix_keys[0], prefix_values[0])
    slot_plus, schemas, lengths = (
        lax.all_to_all(packed(dest_slot + 1), "rep", split_axis=0, concat_axis=0, tiled=True),
        lax.all_to_all(packed(row_schema), "rep", split_axis=0, concat_axis=0, tiled=True),
        lax.all_to_all(packed(suffix_len), "rep", split_axis=0, concat_axis=0, tiled=True),
    )
    target = jnp.arange(row_count) + 1
    matches = slot_plus[None, :] == target[:, None]
    arrived = jnp.sum(jnp.where(matches, jnp.arange(buffer_rows)[None, :], 0), axis=1)
    moved_queries, moved_step_keys, moved_step_values, moved_suffix_keys, moved_suffix_values = (
        lax.all_to_all(packed(queries), "rep", split_axis=0, concat_axis=0, tiled=True),
        lax.all_to_all(packed(step_keys), "rep", split_axis=0, concat_axis=0, tiled=True),
        lax.all_to_all(packed(step_values), "rep", split_axis=0, concat_axis=0, tiled=True),
        lax.all_to_all(packed(suffix_keys), "rep", split_axis=0, concat_axis=0, tiled=True),
        lax.all_to_all(packed(suffix_values), "rep", split_axis=0, concat_axis=0, tiled=True),
    )
    moved_queries = moved_queries[arrived]
    key_rows = jnp.concatenate([moved_suffix_keys[arrived], moved_step_keys[arrived]], axis=1)
    value_rows = jnp.concatenate([moved_suffix_values[arrived], moved_step_values[arrived]], axis=1)
    chosen = held[0][None, :] == schemas[arrived][:, None]
    suffix_scores = local_scores(moved_queries, key_rows, lengths[arrived], suffix_count)
    every_head = lax.all_gather(moved_queries, "tp", axis=2, tiled=True)
    scores = prefix_scores(every_head, prefix_key_rows, chosen)
    schema_max = jnp.max(scores, axis=-1)
    own_wide = jnp.full(schema_max.shape, -jnp.inf, jnp.float32)
    own_wide = lax.dynamic_update_slice_in_dim(
        own_wide, jnp.max(suffix_scores, axis=-1), tp_index * kv_local, 2
    )
    peak_all = lax.pmax(jnp.maximum(schema_max, own_wide), "tp")
    scores, row_peak, peak_all = (
        scores,
        lax.dynamic_slice_in_dim(peak_all, tp_index * kv_local, kv_local, 2),
        peak_all,
    )
    local_weighted, local_totals = local_sums(suffix_scores, row_peak, value_rows)
    weighted, totals = prefix_sums(scores, peak_all, prefix_value_rows, chosen)
    parts_weighted = lax.all_to_all(weighted[None], "tp", split_axis=3, concat_axis=0, tiled=True)
    parts_totals = lax.all_to_all(totals[None], "tp", split_axis=3, concat_axis=0, tiled=True)
    prefix_weighted = jnp.sum(parts_weighted, axis=0)
    prefix_totals = jnp.sum(parts_totals, axis=0)
    result = (prefix_weighted + local_weighted) / (prefix_totals + local_totals)[..., None]
    return result.astype(jnp.bfloat16).reshape(row_count, queries.shape[1], queries.shape[2])


def solution(mesh):
    placed = (
        P("rep", None, "tp"),
        P("rep", None, "tp"),
        P("rep", None, "tp"),
        P("rep", None, "tp"),
        P("rep", None, "tp"),
        P("rep"),
        P("rep"),
        P("rep", None),
        P("rep"),
        P("rep"),
        P("rep", None, "tp", None),
        P("rep", None, "tp", None),
    )
    return jax.shard_map(
        shards, mesh=mesh, in_specs=placed, out_specs=P("rep", None, "tp"), check_vma=False
    )
```

profile of v0, /device:TPU:6, one launch (start us, length us, event | category | flops | bytes accessed | tf_op | source)
XLA Modules:
  0.0 379.7 jit_solution(7269241589955110384)
XLA Ops:
  9.7 10.8 %all-to-all-start.1 = ((s32[64,2,1]{1,2,0:T(1,128)}), s32[64,2,1]{1,2,0:T(1,128)S(1)}, u32[]{:S(2)}, u32[]{:S(2)}) async-start(s32[64,2,1]{1,2,0:T(1,128)} %bitcast.2), calls=%async_computation.1 | async-start | bytes 65536 | tf_op jit(solution)/shard_map/all_to_all | solution.py:104
  22.1 5.9 %all-to-all-done.1 = s32[64,2,1]{1,2,0:T(1,128)S(1)} async-done(((s32[64,2,1]{1,2,0:T(1,128)}), s32[64,2,1]{1,2,0:T(1,128)S(1)}, u32[]{:S(2)}, u32[]{:S(2)}) %all-to-all-start.1) | async-done | bytes 544 | tf_op jit(solution)/shard_map/all_to_all | solution.py:104
  28.0 6.5 %all-to-all-start.3 = ((s32[64,2,1]{1,2,0:T(1,128)}), s32[64,2,1]{1,2,0:T(1,128)S(1)}, u32[]{:S(2)}, u32[]{:S(2)}) async-start(s32[64,2,1]{1,2,0:T(1,128)} %bitcast.12), calls=%async_computation.3 | async-start | bytes 65536 | tf_op jit(solution)/shard_map/all_to_all | solution.py:106
  36.2 5.9 %all-to-all-done.3 = s32[64,2,1]{1,2,0:T(1,128)S(1)} async-done(((s32[64,2,1]{1,2,0:T(1,128)}), s32[64,2,1]{1,2,0:T(1,128)S(1)}, u32[]{:S(2)}, u32[]{:S(2)}) %all-to-all-start.3) | async-done | bytes 544 | tf_op jit(solution)/shard_map/all_to_all | solution.py:106
  42.2 6.5 %all-to-all-start = ((s32[64,2,1]{1,2,0:T(1,128)}), s32[64,2,1]{1,2,0:T(1,128)S(1)}, u32[]{:S(2)}, u32[]{:S(2)}) async-start(s32[64,2,1]{1,2,0:T(1,128)} %bitcast.1), calls=%async_computation | async-start | bytes 65536 | tf_op jit(solution)/shard_map/all_to_all | solution.py:105
  49.3 6.7 %scatter_fusion.2 = bf16[128,2,128]{2,1,0:T(2,128)(2,1)} fusion(bf16[128,2,128]{2,1,0:T(2,128)(2,1)} %broadcast.152.clone.1, s32[64]{0:T(128)S(1)} %get-tuple-element.17, bf16[64,2,128]{2,1,0:T(2,128)(2,1)} %param.13), kind=kCustom, calls=%fused_computation.12 | custom fusion | bytes 98560 | tf_op jit(solution)/shard_map/scatter | solution.py:100
  56.2 10.1 %all-to-all-start.5 = ((bf16[128,2,128]{2,1,0:T(2,128)(2,1)}), bf16[128,2,128]{2,1,0:T(2,128)(2,1)S(1)}, u32[]{:S(2)}, u32[]{:S(2)}) async-start(bf16[128,2,128]{2,1,0:T(2,128)(2,1)} %scatter_fusion.2), calls=%async_computation.5 | async-start | bytes 131072 | tf_op jit(solution)/shard_map/all_to_all | solution.py:113
  67.0 6.8 %scatter_fusion.4 = bf16[128,2,128]{2,1,0:T(2,128)(2,1)} fusion(bf16[128,2,128]{2,1,0:T(2,128)(2,1)} %broadcast.152.clone, s32[64]{0:T(128)S(1)} %get-tuple-element.17, bf16[64,2,128]{2,1,0:T(2,128)(2,1)} %param.14), kind=kCustom, calls=%fused_computation.14 | custom fusion | bytes 98560 | tf_op jit(solution)/shard_map/scatter | solution.py:100
  74.0 10.1 %all-to-all-start.8 = ((bf16[128,2,128]{2,1,0:T(2,128)(2,1)}), bf16[128,2,128]{2,1,0:T(2,128)(2,1)S(1)}, u32[]{:S(2)}, u32[]{:S(2)}) async-start(bf16[128,2,128]{2,1,0:T(2,128)(2,1)} %scatter_fusion.4), calls=%async_computation.8 | async-start | bytes 131072 | tf_op jit(solution)/shard_map/all_to_all | solution.py:114
  85.2 8.1 %scatter_fusion = bf16[128,2,1024]{2,1,0:T(2,128)(2,1)} fusion(bf16[128,2,1024]{2,1,0:T(2,128)(2,1)} %broadcast_in_dim.100, s32[64]{0:T(128)S(1)} %get-tuple-element.17, bf16[64,2,1024]{2,1,0:T(2,128)(2,1)} %param.12), kind=kCustom, calls=%fused_computation.9 | custom fusion | bytes 786688 | tf_op jit(solution)/shard_map/scatter | solution.py:100
  93.3 10.3 %all-to-all-start.2 = ((bf16[128,2,1024]{2,1,0:T(2,128)(2,1)}), bf16[128,2,1024]{2,1,0:T(2,128)(2,1)S(1)}, u32[]{:S(2)}, u32[]{:S(2)}) async-start(bf16[128,2,1024]{2,1,0:T(2,128)(2,1)} %scatter_fusion), calls=%async_computation.2 | async-start | bytes 1048576 | tf_op jit(solution)/shard_map/all_to_all | solution.py:112
  105.5 8.1 %scatter_fusion.1 = bf16[128,64,128]{2,1,0:T(8,128)(2,1)} fusion(bf16[128,64,128]{2,1,0:T(8,128)(2,1)} %broadcast.151.clone.1, s32[64]{0:T(128)S(1)} %get-tuple-element.17, bf16[64,64,128]{2,1,0:T(8,128)(2,1)S(1)} %copy-done.1), kind=kCustom, calls=%fused_computation.11 | custom fusion | bytes 3145984 | tf_op jit(solution)/shard_map/scatter | solution.py:100
  113.6 6.7 %all-to-all-done.2 = bf16[128,2,1024]{2,1,0:T(2,128)(2,1)S(1)} async-done(((bf16[128,2,1024]{2,1,0:T(2,128)(2,1)}), bf16[128,2,1024]{2,1,0:T(2,128)(2,1)S(1)}, u32[]{:S(2)}, u32[]{:S(2)}) %all-to-all-start.2) | async-done | bytes 524320 | tf_op jit(solution)/shard_map/all_to_all | solution.py:112
  120.3 6.9 %all-to-all-start.4 = ((bf16[128,64,128]{2,1,0:T(8,128)(2,1)}), bf16[128,64,128]{2,1,0:T(8,128)(2,1)S(1)}, u32[]{:S(2)}, u32[]{:S(2)}) async-start(bf16[128,64,128]{2,1,0:T(8,128)(2,1)} %scatter_fusion.1), calls=%async_computation.4 | async-start | bytes 4194304 | tf_op jit(solution)/shard_map/all_to_all | solution.py:115
  139.5 9.1 %scatter_fusion.3 = bf16[128,64,128]{2,1,0:T(8,128)(2,1)} fusion(bf16[128,64,128]{2,1,0:T(8,128)(2,1)} %broadcast.151.clone, s32[64]{0:T(128)S(1)} %get-tuple-element.17, bf16[64,64,128]{2,1,0:T(8,128)(2,1)} %param.16), kind=kCustom, calls=%fused_computation.13 | custom fusion | bytes 3145984 | tf_op jit(solution)/shard_map/scatter | solution.py:100
  152.9 23.2 %all-to-all-done.4 = bf16[128,64,128]{2,1,0:T(8,128)(2,1)S(1)} async-done(((bf16[128,64,128]{2,1,0:T(8,128)(2,1)}), bf16[128,64,128]{2,1,0:T(8,128)(2,1)S(1)}, u32[]{:S(2)}, u32[]{:S(2)}) %all-to-all-start.4) | async-done | bytes 2097184 | tf_op jit(solution)/shard_map/all_to_all | solution.py:115
  176.1 8.3 %all-to-all-start.7 = ((bf16[128,64,128]{2,1,0:T(8,128)(2,1)}), bf16[128,64,128]{2,1,0:T(8,128)(2,1)}, u32[]{:S(2)}, u32[]{:S(2)}) async-start(bf16[128,64,128]{2,1,0:T(8,128)(2,1)} %scatter_fusion.3), calls=%async_computation.7 | async-start | bytes 4194304 | tf_op jit(solution)/shard_map/all_to_all | solution.py:116
  200.4 4.6 %bitcast_reduce_fusion = (f32[64,2,8,8]{3,1,0,2:T(2,128)S(1)}, f32[8,64,2,8,256]{4,3,2,1,0:T(8,128)}) fusion(bf16[256,8,128,1,1]{0,2,4,3,1:T(8,128)(2,1)S(1)} %bitcast.102, bf16[64,2,8,8,128]{4,3,2,1,0:T(8,128)(2,1)S(1)} %reshape.318, f32[8,64,2,8,256]{4,3,2,1,0:T(8,128)S(1)} %fusion.13, pred[64]{0:T(512)(128)(4,1)S(1)} %get-tuple-element.12), kind=kOutput, calls=%fused_computation.16 | convolution fusion | flops 545251328 | bytes 19431488 | tf_op jit(solution)/shard_map/rtkgd,pkd->rtkgp/dot_general | solution.py:45
  206.4 41.7 %pmax.7 = f32[64,2,8,8]{3,1,0,2:T(2,128)S(1)} all-reduce(f32[64,2,8,8]{3,1,0,2:T(2,128)S(1)} %max.5), channel_id=1, replica_groups=mesh['rep'=64,'tp'=8] {'tp'}, use_global_device_ids=true, to_apply=%region_10.11 | all-reduce | flops 8192 | bytes 65536 | tf_op jit(solution)/shard_map/pmax | solution.py:130
  248.1 5.8 %convert_reduce_fusion = (f32[64,2,8,8]{3,1,0,2:T(2,128)S(1)}, bf16[64,2,8,8,256]{4,3,1,0,2:T(8,128)(2,1)}) fusion(f32[64,2,8,8]{3,1,0,2:T(2,128)S(1)} %pmax.7, f32[8,64,2,8,256]{4,3,2,1,0:T(8,128)} %get-tuple-element.14), kind=kLoop, calls=%fused_computation.19 | loop fusion | flops 8380416 | bytes 12648448 | tf_op jit(solution)/shard_map/reduce_sum | solution.py:58
  254.8 5.4 %fusion.2 = f32[8,64,2,8,128]{4,3,2,1,0:T(8,128)} fusion(bf16[256,8,128,1,1]{0,2,4,3,1:T(8,128)(2,1)S(1)} %bitcast.105, bf16[64,2,8,8,256]{4,3,1,0,2:T(8,128)(2,1)} %get-tuple-element.6, pred[64]{0:T(512)(128)(4,1)S(1)} %get-tuple-element.12), kind=kOutput, calls=%fused_computation.22 | convolution fusion | flops 538968064 | bytes 8912960 | tf_op jit(solution)/shard_map/rtkgp,pkd->rtkgd/dot_general | solution.py:65
  263.9 6.7 %add_bitcast_fusion = f32[1,64,2,8,8,128]{5,4,2,1,0,3:T(8,128)} fusion(f32[8,64,2,8,128]{4,3,2,1,0:T(8,128)} %fusion.2, bf16[256,8,128,1,1]{0,2,4,3,1:T(8,128)(2,1)S(1)} %bitcast.101, bf16[64,2,8,8,256]{4,3,1,0,2:T(8,128)(2,1)} %get-tuple-element.6, pred[64]{0:T(512)(128)(4,1)S(1)} %get-tuple-element.11), kind=kOutput, calls=%fused_computation.21 | convolution fusion | flops 540016640 | bytes 13107264 | tf_op jit(solution)/shard_map/rtkgp,pkd->rtkgd/dot_general | solution.py:65
  271.9 5.9 %all-to-all-start.6 = ((f32[1,64,2,8,8,128]{5,4,2,1,0,3:T(8,128)}), f32[1,64,2,8,8,128]{5,4,2,1,0,3:T(8,128)}, u32[]{:S(2)}, u32[]{:S(2)}) async-start(f32[1,64,2,8,8,128]{5,4,2,1,0,3:T(8,128)} %add_bitcast_fusion), calls=%async_computation.6 | async-start | bytes 8388608 | tf_op jit(solution)/shard_map/all_to_all | solution.py:138
  282.9 86.2 %all-to-all-done.6 = f32[1,64,2,8,8,128]{5,4,2,1,0,3:T(8,128)} async-done(((f32[1,64,2,8,8,128]{5,4,2,1,0,3:T(8,128)}), f32[1,64,2,8,8,128]{5,4,2,1,0,3:T(8,128)}, u32[]{:S(2)}, u32[]{:S(2)}) %all-to-all-start.6) | async-done | bytes 4194336 | tf_op jit(solution)/shard_map/all_to_all | solution.py:138
  (97 shorter events, 59.4 us)
Async XLA Ops:
  9.7 18.3 %all-to-all-start.1 = ((s32[64,2,1]{1,2,0:T(1,128)}), s32[64,2,1]{1,2,0:T(1,128)S(1)}, u32[]{:S(2)}, u32[]{:S(2)}) async-start(s32[64,2,1]{1,2,0:T(1,128)} %bitcast.2), calls=%async_computation.1 | async-start | bytes 65536 | tf_op jit(solution)/shard_map/all_to_all | solution.py:104
  28.0 14.1 %all-to-all-start.3 = ((s32[64,2,1]{1,2,0:T(1,128)}), s32[64,2,1]{1,2,0:T(1,128)S(1)}, u32[]{:S(2)}, u32[]{:S(2)}) async-start(s32[64,2,1]{1,2,0:T(1,128)} %bitcast.12), calls=%async_computation.3 | async-start | bytes 65536 | tf_op jit(solution)/shard_map/all_to_all | solution.py:106
  42.2 24.1 %copy-start.4 = (s32[64,2,1]{1,2,0:T(1,128)}, s32[64,2,1]{1,2,0:T(1,128)S(1)}, u32[]{:S(2)}) copy-start(s32[64,2,1]{1,2,0:T(1,128)S(1)} %all-to-all-done.3) | copy-start | bytes 1540
  42.2 14.0 %all-to-all-start = ((s32[64,2,1]{1,2,0:T(1,128)}), s32[64,2,1]{1,2,0:T(1,128)S(1)}, u32[]{:S(2)}, u32[]{:S(2)}) async-start(s32[64,2,1]{1,2,0:T(1,128)} %bitcast.1), calls=%async_computation | async-start | bytes 65536 | tf_op jit(solution)/shard_map/all_to_all | solution.py:105
  56.2 10.1 %copy-start.6 = (s32[64,2,1]{1,2,0:T(1,128)}, s32[64,2,1]{1,2,0:T(1,128)S(1)}, u32[]{:S(2)}) copy-start(s32[64,2,1]{1,2,0:T(1,128)S(1)} %all-to-all-done) | copy-start | bytes 1540
  56.2 17.8 %all-to-all-start.5 = ((bf16[128,2,128]{2,1,0:T(2,128)(2,1)}), bf16[128,2,128]{2,1,0:T(2,128)(2,1)S(1)}, u32[]{:S(2)}, u32[]{:S(2)}) async-start(bf16[128,2,128]{2,1,0:T(2,128)(2,1)} %scatter_fusion.2), calls=%async_computation.5 | async-start | bytes 131072 | tf_op jit(solution)/shard_map/all_to_all | solution.py:113
  67.0 38.5 %copy-start.1 = (bf16[64,64,128]{2,1,0:T(8,128)(2,1)S(1)}, bf16[64,64,128]{2,1,0:T(8,128)(2,1)}, u32[]{:S(2)}) copy-start(bf16[64,64,128]{2,1,0:T(8,128)(2,1)} %param.15) | copy-start | bytes 3145732
  74.0 19.2 %all-to-all-start.8 = ((bf16[128,2,128]{2,1,0:T(2,128)(2,1)}), bf16[128,2,128]{2,1,0:T(2,128)(2,1)S(1)}, u32[]{:S(2)}, u32[]{:S(2)}) async-start(bf16[128,2,128]{2,1,0:T(2,128)(2,1)} %scatter_fusion.4), calls=%async_computation.8 | async-start | bytes 131072 | tf_op jit(solution)/shard_map/all_to_all | solution.py:114
  93.3 27.0 %all-to-all-start.2 = ((bf16[128,2,1024]{2,1,0:T(2,128)(2,1)}), bf16[128,2,1024]{2,1,0:T(2,128)(2,1)S(1)}, u32[]{:S(2)}, u32[]{:S(2)}) async-start(bf16[128,2,1024]{2,1,0:T(2,128)(2,1)} %scatter_fusion), calls=%async_computation.2 | async-start | bytes 1048576 | tf_op jit(solution)/shard_map/all_to_all | solution.py:112
  120.3 55.8 %all-to-all-start.4 = ((bf16[128,64,128]{2,1,0:T(8,128)(2,1)}), bf16[128,64,128]{2,1,0:T(8,128)(2,1)S(1)}, u32[]{:S(2)}, u32[]{:S(2)}) async-start(bf16[128,64,128]{2,1,0:T(8,128)(2,1)} %scatter_fusion.1), calls=%async_computation.4 | async-start | bytes 4194304 | tf_op jit(solution)/shard_map/all_to_all | solution.py:115
  127.2 67.6 %all-gather.3.cloned.1.call-start = ((), (), s32[]{:S(2)}) async-start(), calls=%async_computation.10 | async-start | bytes 2359296 | tf_op jit(solution)/shard_map/all_gather | solution.py:123
  137.7 12.0 %copy-start.5 = (s32[64,2,1]{1,2,0:T(1,128)S(1)}, s32[64,2,1]{1,2,0:T(1,128)}, u32[]{:S(2)}) copy-start(s32[64,2,1]{1,2,0:T(1,128)} %copy-done.4) | copy-start | bytes 1540
  139.5 11.8 %copy-start.7 = (s32[64,2,1]{1,2,0:T(1,128)S(1)}, s32[64,2,1]{1,2,0:T(1,128)}, u32[]{:S(2)}) copy-start(s32[64,2,1]{1,2,0:T(1,128)} %copy-done.6) | copy-start | bytes 1540
  152.1 35.6 %copy-start = (bf16[64,2,1024]{2,1,0:T(2,128)(2,1)S(1)}, bf16[64,2,1024]{2,1,0:T(2,128)(2,1)}, u32[]{:S(2)}) copy-start(bf16[64,2,1024]{2,1,0:T(2,128)(2,1)} %gather_fusion.1) | copy-start | bytes 786436
  152.9 31.5 %copy-start.10 = (s32[1,2]{1,0:T(1,128)S(1)}, s32[1,2]{1,0:T(1,128)}, u32[]{:S(2)}) copy-start(s32[1,2]{1,0:T(1,128)} %param.19) | copy-start | bytes 28
  176.1 84.2 %all-to-all-start.7 = ((bf16[128,64,128]{2,1,0:T(8,128)(2,1)}), bf16[128,64,128]{2,1,0:T(8,128)(2,1)}, u32[]{:S(2)}, u32[]{:S(2)}) async-start(bf16[128,64,128]{2,1,0:T(8,128)(2,1)} %scatter_fusion.3), calls=%async_computation.7 | async-start | bytes 4194304 | tf_op jit(solution)/shard_map/all_to_all | solution.py:116
  187.8 2.6 copy-start.8
  187.8 2.6 copy-start.9
  248.1 6.7 %copy-start.3 = (bf16[1,1,256,1024]{2,3,1,0:T(8,128)(2,1)S(1)}, bf16[1,1,256,1024]{2,3,1,0:T(8,128)(2,1)}, u32[]{:S(2)}) copy-start(bf16[1,1,256,1024]{2,3,1,0:T(8,128)(2,1)} %copy.113) | copy-start | bytes 1572868
  260.3 11.7 %all-to-all-start.9 = ((f32[8,1,1024]{2,1,0:T(1,128)}), f32[8,1,1024]{2,1,0:T(1,128)S(1)}, u32[]{:S(2)}, u32[]{:S(2)}) async-start(f32[8,1,1024]{2,1,0:T(1,128)} %reshape.348), calls=%async_computation.9 | async-start | bytes 65536 | tf_op jit(solution)/shard_map/all_to_all | solution.py:139
  271.9 97.1 %all-to-all-start.6 = ((f32[1,64,2,8,8,128]{5,4,2,1,0,3:T(8,128)}), f32[1,64,2,8,8,128]{5,4,2,1,0,3:T(8,128)}, u32[]{:S(2)}, u32[]{:S(2)}) async-start(f32[1,64,2,8,8,128]{5,4,2,1,0,3:T(8,128)} %add_bitcast_fusion), calls=%async_computation.6 | async-start | bytes 8388608 | tf_op jit(solution)/shard_map/all_to_all | solution.py:138
  277.9 3.0 copy-start.2
Sparse Core Ops, SparseCore 0:
  131.0 54.5 all-gather.2
where the time goes:
time: 382 us; the launch traced here: 380 us
  waiting for transfers between devices  130 us (34%)
  starting transfers between devices  79.3 us (21%)
  local copies, waits for them, and re-layouts  75.1 us (20%)
  blocking collectives  41.7 us (11%)
  matrix products  22.4 us (6%)
  other arithmetic  17.7 us (5%)
  between operations  13.8 us (4%)
    all_to_all x1, waiting for transfers between devices, shards(): lax.all_to_all(weighted[None], 'tp', split_axis=3, concat_axis=0, tiled=T...  86.2 us
    pmax x1, blocking collectives, shards(): peak_all = lax.pmax(jnp.maximum(schema_max, own_wide), 'tp')  41.7 us
    scatter x8, local copies, waits for them, and re-layouts, packed(): jnp.zeros((buffer_rows,) + values.shape[1:], values.dtype).at[placed]  41.4 us
    all_to_all x1, waiting for transfers between devices, shards(): lax.all_to_all(packed(suffix_keys), 'rep', split_axis=0, concat_axis=0, t...  23.2 us
    dot_general x2, matrix products, prefix_sums(): jnp.einsum('rtkgp,pkd->rtkgd', masked, value_heads, preferred_element_typ...  12.2 us
    all_to_all x1, starting transfers between devices, shards(): lax.all_to_all(packed(dest_slot + 1), 'rep', split_axis=0, concat_axis=0,...  10.8 us
    all_to_all x1, starting transfers between devices, shards(): lax.all_to_all(packed(queries), 'rep', split_axis=0, concat_axis=0, tiled...  10.3 us
    all_to_all x1, starting transfers between devices, shards(): lax.all_to_all(packed(step_keys), 'rep', split_axis=0, concat_axis=0, til...  10.1 us
  transfers between devices with their start and end apart: 11, of which 8 were waited for; matrix products, arithmetic and copies ran while one was open for 28% of the time, Pallas kernels for 0%

commit v1 on v0

--- a/solution.py
+++ b/solution.py
@@ -36,36 +36,26 @@
 
 def prefix_scores(query_rows, prefix_block, chosen):
     row_count, step_count, width = query_rows.shape
+    slot_count, token_count = prefix_block.shape[0], prefix_block.shape[1]
     kv_count = prefix_block.shape[2] // HD
     group_size = width // HD // kv_count
     query_heads = query_rows.reshape(row_count, step_count, kv_count, group_size, HD)
-    combined = None
-    for slot_index in range(prefix_block.shape[0]):
-        key_heads = prefix_block[slot_index].reshape(prefix_block.shape[1], kv_count, HD)
-        scores = jnp.einsum(
-            "rtkgd,pkd->rtkgp", query_heads, key_heads, preferred_element_type=jnp.float32
-        ) * HD ** (-0.5)
-        if combined is None:
-            combined = scores
-        else:
-            combined = jnp.where(chosen[:, slot_index][:, None, None, None, None], scores, combined)
-    return combined
+    key_heads = prefix_block.reshape(slot_count * token_count, kv_count, HD)
+    scores = jnp.einsum(
+        "rtkgd,pkd->rtkgp", query_heads, key_heads, preferred_element_type=jnp.float32
+    ) * HD ** (-0.5)
+    allowed = jnp.repeat(chosen, token_count, axis=1)
+    return jnp.where(allowed[:, None, None, None, :], scores, -jnp.inf)
 
 
 def prefix_sums(scores, row_peak, value_block, chosen):
     kv_count = value_block.shape[2] // HD
     weights = jnp.exp(scores - row_peak[..., None]).astype(jnp.bfloat16)
     totals = jnp.sum(weights.astype(jnp.float32), axis=-1)
-    weighted = None
-    for slot_index in range(value_block.shape[0]):
-        value_heads = value_block[slot_index].reshape(value_block.shape[1], kv_count, HD)
-        masked = jnp.where(
-            chosen[:, slot_index][:, None, None, None, None], weights, jnp.zeros_like(weights)
-        )
-        term = jnp.einsum(
-            "rtkgp,pkd->rtkgd", masked, value_heads, preferred_element_type=jnp.float32
-        )
-        weighted = term if weighted is None else weighted + term
+    value_heads = value_block.reshape(value_block.shape[0] * value_block.shape[1], kv_count, HD)
+    weighted = jnp.einsum(
+        "rtkgp,pkd->rtkgd", weights, value_heads, preferred_element_type=jnp.float32
+    )
     return (weighted, totals)
 
 
@@ -100,11 +90,9 @@
         return jnp.zeros((buffer_rows,) + values.shape[1:], values.dtype).at[placed].set(values)
 
     prefix_key_rows, prefix_value_rows = (prefix_keys[0], prefix_values[0])
-    slot_plus, schemas, lengths = (
-        lax.all_to_all(packed(dest_slot + 1), "rep", split_axis=0, concat_axis=0, tiled=True),
-        lax.all_to_all(packed(row_schema), "rep", split_axis=0, concat_axis=0, tiled=True),
-        lax.all_to_all(packed(suffix_len), "rep", split_axis=0, concat_axis=0, tiled=True),
-    )
+    row_facts = jnp.stack([dest_slot + 1, row_schema, suffix_len], axis=1)
+    row_facts = lax.all_to_all(packed(row_facts), "rep", split_axis=0, concat_axis=0, tiled=True)
+    slot_plus, schemas, lengths = (row_facts[:, 0], row_facts[:, 1], row_facts[:, 2])
     target = jnp.arange(row_count) + 1
     matches = slot_plus[None, :] == target[:, None]
     arrived = jnp.sum(jnp.where(matches, jnp.arange(buffer_rows)[None, :], 0), axis=1)

time: 382 us -> 361 us (0.945)
  starting transfers between devices: 79.3 us -> 67.3 us
  local copies, waits for them, and re-layouts: 75.1 us -> 69.2 us
    all_to_all x3 -> x1, starting transfers between devices: 23.9 us -> 10.8 us  [shards(): lax.all_to_all(packed(row_facts), 'rep', split_axis=0, concat_axis=0, til...]
    all_to_all x1, waiting for transfers between devices: 23.2 us -> 35.7 us  [shards(): lax.all_to_all(packed(suffix_keys), 'rep', split_axis=0, concat_axis=0, t...]
    all_to_all x3 -> x1, waiting for transfers between devices: 12 us -> 0.42 us  [shards(): lax.all_to_all(packed(row_facts), 'rep', split_axis=0, concat_axis=0, til...]
    dot_general x2 -> x1, matrix products: 12.2 us -> 9.17 us  [prefix_sums(): jnp.einsum('rtkgp,pkd->rtkgd', weights, value_heads, preferred_element_ty...]
    scatter x8 -> x6, local copies, waits for them, and re-layouts: 41.4 us -> 40.2 us  [packed(): jnp.zeros((buffer_rows,) + values.shape[1:], values.dtype).at[placed]]
  transfers between devices with their start and end apart: 11 -> 9, of which waited for: 8 -> 5; matrix products, arithmetic and copies ran while one was open for 28% -> 27% of each run, Pallas kernels for 0% -> 0%
where the time goes in v1:
time: 361 us; the launch traced here: 359 us
  waiting for transfers between devices  129 us (36%)
  local copies, waits for them, and re-layouts  69.2 us (19%)
  starting transfers between devices  67.3 us (19%)
  blocking collectives  41.5 us (11%)
  matrix products  20 us (6%)
  other arithmetic  18.1 us (5%)
  between operations  13.7 us (4%)
    all_to_all x1, waiting for transfers between devices, shards(): lax.all_to_all(weighted[None], 'tp', split_axis=3, concat_axis=0, tiled=T...  85.8 us
    pmax x1, blocking collectives, shards(): peak_all = lax.pmax(jnp.maximum(schema_max, own_wide), 'tp')  41.5 us
    scatter x6, local copies, waits for them, and re-layouts, packed(): jnp.zeros((buffer_rows,) + values.shape[1:], values.dtype).at[placed]  40.2 us
    all_to_all x1, waiting for transfers between devices, shards(): lax.all_to_all(packed(suffix_keys), 'rep', split_axis=0, concat_axis=0, t...  35.7 us
    all_to_all x1, starting transfers between devices, shards(): lax.all_to_all(packed(row_facts), 'rep', split_axis=0, concat_axis=0, til...  10.8 us
    all_to_all x1, starting transfers between devices, shards(): lax.all_to_all(packed(queries), 'rep', split_axis=0, concat_axis=0, tiled...  10.3 us
    all_to_all x1, starting transfers between devices, shards(): lax.all_to_all(packed(step_values), 'rep', split_axis=0, concat_axis=0, t...  10 us
    all_to_all x1, starting transfers between devices, shards(): lax.all_to_all(packed(step_keys), 'rep', split_axis=0, concat_axis=0, til...  9.91 us
  transfers between devices with their start and end apart: 9, of which 5 were waited for; matrix products, arithmetic and copies ran while one was open for 27% of the time, Pallas kernels for 0%

profile of v1, /device:TPU:6, one launch (start us, length us, event | category | flops | bytes accessed | tf_op | source)
XLA Modules:
  0.0 358.7 jit_solution(766932302193895828)
XLA Ops:
  10.9 10.8 %all-to-all-start = ((s32[64,2,3]{2,1,0:T(2,128)}), s32[64,2,3]{2,1,0:T(2,128)S(1)}, u32[]{:S(2)}, u32[]{:S(2)}) async-start(s32[64,2,3]{2,1,0:T(2,128)} %bitcast.4), calls=%async_computation | async-start | bytes 131072 | tf_op jit(solution)/shard_map/all_to_all | solution.py:94
  22.4 6.7 %scatter_fusion.2 = bf16[128,2,128]{2,1,0:T(2,128)(2,1)} fusion(bf16[128,2,128]{2,1,0:T(2,128)(2,1)} %broadcast.142.clone.1, s32[64]{0:T(128)S(1)} %compare_select_fusion.1, bf16[64,2,128]{2,1,0:T(2,128)(2,1)} %param.13), kind=kCustom, calls=%fused_computation.10 | custom fusion | bytes 98560 | tf_op jit(solution)/shard_map/scatter | solution.py:90
  29.5 9.9 %all-to-all-start.3 = ((bf16[128,2,128]{2,1,0:T(2,128)(2,1)}), bf16[128,2,128]{2,1,0:T(2,128)(2,1)S(1)}, u32[]{:S(2)}, u32[]{:S(2)}) async-start(bf16[128,2,128]{2,1,0:T(2,128)(2,1)} %scatter_fusion.2), calls=%async_computation.3 | async-start | bytes 131072 | tf_op jit(solution)/shard_map/all_to_all | solution.py:101
  40.1 6.8 %scatter_fusion.4 = bf16[128,2,128]{2,1,0:T(2,128)(2,1)} fusion(bf16[128,2,128]{2,1,0:T(2,128)(2,1)} %broadcast.142.clone, s32[64]{0:T(128)S(1)} %compare_select_fusion.1, bf16[64,2,128]{2,1,0:T(2,128)(2,1)} %param.14), kind=kCustom, calls=%fused_computation.12 | custom fusion | bytes 98560 | tf_op jit(solution)/shard_map/scatter | solution.py:90
  47.8 10.0 %all-to-all-start.6 = ((bf16[128,2,128]{2,1,0:T(2,128)(2,1)}), bf16[128,2,128]{2,1,0:T(2,128)(2,1)S(1)}, u32[]{:S(2)}, u32[]{:S(2)}) async-start(bf16[128,2,128]{2,1,0:T(2,128)(2,1)} %scatter_fusion.4), calls=%async_computation.6 | async-start | bytes 131072 | tf_op jit(solution)/shard_map/all_to_all | solution.py:102
  58.9 8.1 %scatter_fusion = bf16[128,2,1024]{2,1,0:T(2,128)(2,1)} fusion(bf16[128,2,1024]{2,1,0:T(2,128)(2,1)} %broadcast_in_dim.92, s32[64]{0:T(128)S(1)} %compare_select_fusion.1, bf16[64,2,1024]{2,1,0:T(2,128)(2,1)} %param.12), kind=kCustom, calls=%fused_computation.8 | custom fusion | bytes 786688 | tf_op jit(solution)/shard_map/scatter | solution.py:90
  67.0 10.3 %all-to-all-start.1 = ((bf16[128,2,1024]{2,1,0:T(2,128)(2,1)}), bf16[128,2,1024]{2,1,0:T(2,128)(2,1)S(1)}, u32[]{:S(2)}, u32[]{:S(2)}) async-start(bf16[128,2,1024]{2,1,0:T(2,128)(2,1)} %scatter_fusion), calls=%async_computation.1 | async-start | bytes 1048576 | tf_op jit(solution)/shard_map/all_to_all | solution.py:100
  79.2 8.1 %scatter_fusion.1 = bf16[128,64,128]{2,1,0:T(8,128)(2,1)} fusion(bf16[128,64,128]{2,1,0:T(8,128)(2,1)} %broadcast.141.clone.1, s32[64]{0:T(128)S(1)} %compare_select_fusion.1, bf16[64,64,128]{2,1,0:T(8,128)(2,1)S(1)} %copy-done.1), kind=kCustom, calls=%fused_computation.9 | custom fusion | bytes 3145984 | tf_op jit(solution)/shard_map/scatter | solution.py:90
  87.3 6.7 %all-to-all-done.1 = bf16[128,2,1024]{2,1,0:T(2,128)(2,1)S(1)} async-done(((bf16[128,2,1024]{2,1,0:T(2,128)(2,1)}), bf16[128,2,1024]{2,1,0:T(2,128)(2,1)S(1)}, u32[]{:S(2)}, u32[]{:S(2)}) %all-to-all-start.1) | async-done | bytes 524320 | tf_op jit(solution)/shard_map/all_to_all | solution.py:100
  94.0 6.9 %all-to-all-start.2 = ((bf16[128,64,128]{2,1,0:T(8,128)(2,1)}), bf16[128,64,128]{2,1,0:T(8,128)(2,1)S(1)}, u32[]{:S(2)}, u32[]{:S(2)}) async-start(bf16[128,64,128]{2,1,0:T(8,128)(2,1)} %scatter_fusion.1), calls=%async_computation.2 | async-start | bytes 4194304 | tf_op jit(solution)/shard_map/all_to_all | solution.py:103
  105.1 9.1 %scatter_fusion.3 = bf16[128,64,128]{2,1,0:T(8,128)(2,1)} fusion(bf16[128,64,128]{2,1,0:T(8,128)(2,1)} %broadcast.141.clone, s32[64]{0:T(128)S(1)} %compare_select_fusion.1, bf16[64,64,128]{2,1,0:T(8,128)(2,1)} %param.16), kind=kCustom, calls=%fused_computation.11 | custom fusion | bytes 3145984 | tf_op jit(solution)/shard_map/scatter | solution.py:90
  114.2 35.7 %all-to-all-done.2 = bf16[128,64,128]{2,1,0:T(8,128)(2,1)S(1)} async-done(((bf16[128,64,128]{2,1,0:T(8,128)(2,1)}), bf16[128,64,128]{2,1,0:T(8,128)(2,1)S(1)}, u32[]{:S(2)}, u32[]{:S(2)}) %all-to-all-start.2) | async-done | bytes 2097184 | tf_op jit(solution)/shard_map/all_to_all | solution.py:103
  149.8 8.3 %all-to-all-start.5 = ((bf16[128,64,128]{2,1,0:T(8,128)(2,1)}), bf16[128,64,128]{2,1,0:T(8,128)(2,1)}, u32[]{:S(2)}, u32[]{:S(2)}) async-start(bf16[128,64,128]{2,1,0:T(8,128)(2,1)} %scatter_fusion.3), calls=%async_computation.5 | async-start | bytes 4194304 | tf_op jit(solution)/shard_map/all_to_all | solution.py:104
  159.7 2.5 copy.83
  169.6 2.8 fusion.25
  174.0 3.3 reshape.284
  177.4 7.5 %bitcast_reduce_fusion = (f32[64,2,8,8]{3,1,0,2:T(2,128)S(1)}, f32[8,64,2,8,512]{4,3,2,1,0:T(8,128)}) fusion(pred[64,512]{1,0:T(8,128)(4,1)S(1)} %bitcast.100, bf16[512,8,128,1,1]{2,1,0,4,3:T(8,128)(2,1)S(1)} %bitcast.94, bf16[64,2,8,8,128]{4,3,2,1,0:T(8,128)(2,1)S(1)} %reshape.284), kind=kOutput, calls=%fused_computation.14 | convolution fusion | flops 1086316544 | bytes 19988480 | tf_op jit(solution)/shard_map/rtkgd,pkd->rtkgp/dot_general | solution.py:44
  186.2 41.5 %pmax.7 = f32[64,2,8,8]{3,1,0,2:T(2,128)S(1)} all-reduce(f32[64,2,8,8]{3,1,0,2:T(2,128)S(1)} %max.5), channel_id=1, replica_groups=mesh['rep'=64,'tp'=8] {'tp'}, use_global_device_ids=true, to_apply=%region_8.9 | all-reduce | flops 8192 | bytes 65536 | tf_op jit(solution)/shard_map/pmax | solution.py:118
  227.7 8.5 %convert_reduce_fusion = f32[64,2,8,8]{3,1,0,2:T(2,128)S(1)} fusion(f32[64,2,8,8]{3,1,0,2:T(2,128)S(1)} %pmax.7, f32[8,64,2,8,512]{4,3,2,1,0:T(8,128)} %get-tuple-element.9, pred[64,512]{1,0:T(8,128)(4,1)S(1)} %bitcast.101), kind=kLoop, calls=%fused_computation.17 | loop fusion | flops 25157632 | bytes 16875520 | tf_op jit(solution)/shard_map/reduce_sum | solution.py:54
  237.2 3.6 %all-to-all-start.7 = ((f32[8,1,1024]{2,1,0:T(1,128)}), f32[8,1,1024]{2,1,0:T(1,128)S(1)}, u32[]{:S(2)}, u32[]{:S(2)}) async-start(f32[8,1,1024]{2,1,0:T(1,128)} %reshape.287), calls=%async_computation.7 | async-start | bytes 65536 | tf_op jit(solution)/shard_map/all_to_all | solution.py:127
  240.8 9.2 %convolution_bitcast_fusion = f32[1,64,2,8,8,128]{5,4,2,1,0,3:T(8,128)} fusion(bf16[512,8,128,1,1]{2,1,0,4,3:T(8,128)(2,1)S(1)} %bitcast.99, f32[8,64,2,8,512]{4,3,2,1,0:T(8,128)} %get-tuple-element.9, f32[64,2,8,8]{3,1,0,2:T(2,128)S(1)} %pmax.7, pred[64,512]{1,0:T(8,128)(4,1)S(1)} %bitcast.102), kind=kOutput, calls=%fused_computation.19 | convolution fusion | flops 1090519040 | bytes 22085632 | tf_op jit(solution)/shard_map/rtkgp,pkd->rtkgd/dot_general | solution.py:56
  250.0 7.3 %all-to-all-start.4 = ((f32[1,64,2,8,8,128]{5,4,2,1,0,3:T(8,128)}), f32[1,64,2,8,8,128]{5,4,2,1,0,3:T(8,128)}, u32[]{:S(2)}, u32[]{:S(2)}) async-start(f32[1,64,2,8,8,128]{5,4,2,1,0,3:T(8,128)} %convolution_bitcast_fusion), calls=%async_computation.4 | async-start | bytes 8388608 | tf_op jit(solution)/shard_map/all_to_all | solution.py:126
  262.3 85.8 %all-to-all-done.4 = f32[1,64,2,8,8,128]{5,4,2,1,0,3:T(8,128)} async-done(((f32[1,64,2,8,8,128]{5,4,2,1,0,3:T(8,128)}), f32[1,64,2,8,8,128]{5,4,2,1,0,3:T(8,128)}, u32[]{:S(2)}, u32[]{:S(2)}) %all-to-all-start.4) | async-done | bytes 4194336 | tf_op jit(solution)/shard_map/all_to_all | solution.py:126
  348.1 2.5 reduce_sum.61
  (77 shorter events, 32.9 us)
Async XLA Ops:
  6.5 72.6 %copy-start.1 = (bf16[64,64,128]{2,1,0:T(8,128)(2,1)S(1)}, bf16[64,64,128]{2,1,0:T(8,128)(2,1)}, u32[]{:S(2)}) copy-start(bf16[64,64,128]{2,1,0:T(8,128)(2,1)} %param.15) | copy-start | bytes 3145732
  10.9 18.6 %all-to-all-start = ((s32[64,2,3]{2,1,0:T(2,128)}), s32[64,2,3]{2,1,0:T(2,128)S(1)}, u32[]{:S(2)}, u32[]{:S(2)}) async-start(s32[64,2,3]{2,1,0:T(2,128)} %bitcast.4), calls=%async_computation | async-start | bytes 131072 | tf_op jit(solution)/shard_map/all_to_all | solution.py:94
  29.5 17.7 %all-to-all-start.3 = ((bf16[128,2,128]{2,1,0:T(2,128)(2,1)}), bf16[128,2,128]{2,1,0:T(2,128)(2,1)S(1)}, u32[]{:S(2)}, u32[]{:S(2)}) async-start(bf16[128,2,128]{2,1,0:T(2,128)(2,1)} %scatter_fusion.2), calls=%async_computation.3 | async-start | bytes 131072 | tf_op jit(solution)/shard_map/all_to_all | solution.py:101
  47.2 0.6 copy-start.6
  47.8 19.2 %all-to-all-start.6 = ((bf16[128,2,128]{2,1,0:T(2,128)(2,1)}), bf16[128,2,128]{2,1,0:T(2,128)(2,1)S(1)}, u32[]{:S(2)}, u32[]{:S(2)}) async-start(bf16[128,2,128]{2,1,0:T(2,128)(2,1)} %scatter_fusion.4), calls=%async_computation.6 | async-start | bytes 131072 | tf_op jit(solution)/shard_map/all_to_all | solution.py:102
  67.0 27.0 %copy-start.4 = (bf16[128,2,128]{2,1,0:T(2,128)(2,1)}, bf16[128,2,128]{2,1,0:T(2,128)(2,1)S(1)}, u32[]{:S(2)}) copy-start(bf16[128,2,128]{2,1,0:T(2,128)(2,1)S(1)} %all-to-all-done.6) | copy-start | bytes 196612
  67.0 27.0 %all-to-all-start.1 = ((bf16[128,2,1024]{2,1,0:T(2,128)(2,1)}), bf16[128,2,1024]{2,1,0:T(2,128)(2,1)S(1)}, u32[]{:S(2)}, u32[]{:S(2)}) async-start(bf16[128,2,1024]{2,1,0:T(2,128)(2,1)} %scatter_fusion), calls=%async_computation.1 | async-start | bytes 1048576 | tf_op jit(solution)/shard_map/all_to_all | solution.py:100
  94.0 55.8 %all-to-all-start.2 = ((bf16[128,64,128]{2,1,0:T(8,128)(2,1)}), bf16[128,64,128]{2,1,0:T(8,128)(2,1)S(1)}, u32[]{:S(2)}, u32[]{:S(2)}) async-start(bf16[128,64,128]{2,1,0:T(8,128)(2,1)} %scatter_fusion.1), calls=%async_computation.2 | async-start | bytes 4194304 | tf_op jit(solution)/shard_map/all_to_all | solution.py:103
  100.9 73.1 %all-gather.3.cloned.1.call-start = ((), (), s32[]{:S(2)}) async-start(), calls=%async_computation.8 | async-start | bytes 2359296 | tf_op jit(solution)/shard_map/all_gather | solution.py:111
  114.2 50.3 %copy-start.7 = (s32[1,2]{1,0:T(1,128)S(1)}, s32[1,2]{1,0:T(1,128)}, u32[]{:S(2)}) copy-start(s32[1,2]{1,0:T(1,128)} %param.19) | copy-start | bytes 28
  114.2 52.9 %copy-start = (bf16[64,2,1024]{2,1,0:T(2,128)(2,1)S(1)}, bf16[64,2,1024]{2,1,0:T(2,128)(2,1)}, u32[]{:S(2)}) copy-start(bf16[64,2,1024]{2,1,0:T(2,128)(2,1)} %gather_fusion.1) | copy-start | bytes 786436
  149.8 87.3 %all-to-all-start.5 = ((bf16[128,64,128]{2,1,0:T(8,128)(2,1)}), bf16[128,64,128]{2,1,0:T(8,128)(2,1)}, u32[]{:S(2)}, u32[]{:S(2)}) async-start(bf16[128,64,128]{2,1,0:T(8,128)(2,1)} %scatter_fusion.3), calls=%async_computation.5 | async-start | bytes 4194304 | tf_op jit(solution)/shard_map/all_to_all | solution.py:104
  227.7 13.1 %copy-start.2 = (bf16[64,8,8,128]{3,2,1,0:T(8,128)(2,1)S(1)}, bf16[64,8,8,128]{3,2,1,0:T(8,128)(2,1)}, u32[]{:S(2)}) copy-start(bf16[64,8,8,128]{3,2,1,0:T(8,128)(2,1)} %copy.83) | copy-start | bytes 3145732
  237.2 12.8 %all-to-all-start.7 = ((f32[8,1,1024]{2,1,0:T(1,128)}), f32[8,1,1024]{2,1,0:T(1,128)S(1)}, u32[]{:S(2)}, u32[]{:S(2)}) async-start(f32[8,1,1024]{2,1,0:T(1,128)} %reshape.287), calls=%async_computation.7 | async-start | bytes 65536 | tf_op jit(solution)/shard_map/all_to_all | solution.py:127
  250.0 7.4 %copy-start.5 = (bf16[128,2,128]{2,1,0:T(2,128)(2,1)S(1)}, bf16[128,2,128]{2,1,0:T(2,128)(2,1)}, u32[]{:S(2)}) copy-start(bf16[128,2,128]{2,1,0:T(2,128)(2,1)} %copy-done.4) | copy-start | bytes 196612
  250.0 10.4 %copy-start.3 = (f32[64,2,1,8,66]{4,3,1,0,2:T(8,128)S(1)}, f32[64,2,1,8,66]{4,3,1,0,2:T(8,128)}, u32[]{:S(2)}) copy-start(f32[64,2,1,8,66]{4,3,1,0,2:T(8,128)} %get-tuple-element.11) | copy-start | bytes 811012
  250.0 98.1 %all-to-all-start.4 = ((f32[1,64,2,8,8,128]{5,4,2,1,0,3:T(8,128)}), f32[1,64,2,8,8,128]{5,4,2,1,0,3:T(8,128)}, u32[]{:S(2)}, u32[]{:S(2)}) async-start(f32[1,64,2,8,8,128]{5,4,2,1,0,3:T(8,128)} %convolution_bitcast_fusion), calls=%async_computation.4 | async-start | bytes 8388608 | tf_op jit(solution)/shard_map/all_to_all | solution.py:126
Sparse Core Ops, SparseCore 0:
  103.8 54.5 all-gather.2
